TPU v7x, 32 devices: a whole 2x2x4 slice. The times are simulated.
32 devices in a mesh: gx: 2 (over y), gy: 4 (over x, core), gz: 4 (over z).
Axes of the slice: x: 2, y: 2, z: 4, core: 2. Of those that a mesh axis runs over, the one named last changes fastest.
Arguments:
- snapshot: float32 [12, 1024, 8, 512], P(None, 'gz', 'gx', 'gy'), may hold values from -108 to 108
- species_pick: int32 [8], replicated, may hold values from 0 to 11, as said below
- basis_start: float32 [1024, 384], replicated, may hold values from -0.1875 to 0.1875
Outputs:
- gram_matrix: float32 [1024, 1024], P(('gx', 'gy', 'gz'))
- basis: float32 [1024, 384], P(('gx', 'gy', 'gz'))
- core_tensor: float32 [8, 384, 8, 512], P(None, None, ('gx', 'gz'), 'gy')
Inputs may be any that keep to these rules, and one draw needn't show every extreme that they name: `species_pick`: 8 distinct species numbers; 0 and 11 are always among them.
All inputs are finite; a program needn't handle non-finite values.
Results may differ from a plain program's by a relative error of at most 0.0003.
Values sent between devices are 32-bit elements; how exact they have to be, the bound alone decides.
A program may use at most 128 MiB of HBM per device.

v0:
```python
import jax
import jax.numpy as jnp
from jax import lax
from jax.sharding import PartitionSpec as P


def per_device(snapshot, species_pick, basis_start):
    highest = lax.Precision.HIGHEST
    picked = jnp.take(snapshot, species_pick, axis=0)
    full_panel = lax.all_to_all(picked, "gz", split_axis=2, concat_axis=1, tiled=True)
    total_rows = full_panel.shape[1]
    column_total = (
        full_panel.shape[0]
        * full_panel.shape[2]
        * lax.axis_size("gz")
        * lax.axis_size("gx")
        * full_panel.shape[3]
        * lax.axis_size("gy")
    )
    scaling = 1.0 / column_total
    row_share = total_rows // lax.axis_size(("gx", "gy", "gz"))
    gram_full = lax.psum(
        jnp.einsum("sxyz,swyz->xw", full_panel, full_panel, precision=highest) * scaling,
        ("gx", "gy", "gz"),
    )
    image_full = jnp.dot(gram_full, basis_start, precision=highest)
    inner_gram = jnp.einsum("xr,xq->rq", image_full, image_full, precision=highest)
    lower_factor = jnp.linalg.cholesky(inner_gram)
    basis_full = jax.scipy.linalg.solve_triangular(lower_factor, image_full.T, lower=True).T
    offset = lax.axis_index(("gx", "gy", "gz")) * row_share
    gram_rows = lax.dynamic_slice_in_dim(gram_full, offset, row_share, 0)
    basis_rows = lax.dynamic_slice_in_dim(basis_full, offset, row_share, 0)
    local_rows = picked.shape[1]
    own_rows = lax.dynamic_slice_in_dim(
        basis_full, lax.axis_index("gz") * local_rows, local_rows, 0
    )
    projected = jnp.einsum("xr,sxyz->sryz", own_rows, picked, precision=highest)
    core_out = lax.psum_scatter(projected, "gz", scatter_dimension=2, tiled=True)
    return (gram_rows, basis_rows, core_out)


def solution(mesh):
    return jax.shard_map(
        per_device,
        mesh=mesh,
        in_specs=(P(None, "gz", "gx", "gy"), P(), P()),
        out_specs=(
            P(("gx", "gy", "gz"), None),
            P(("gx", "gy", "gz"), None),
            P(None, None, ("gx", "gz"), "gy"),
        ),
        check_vma=False,
    )
```

profile of v0, /device:TPU:0, one launch (start us, length us, event | category | flops | bytes accessed | tf_op | source)
XLA Modules:
  0.0 657.8 jit_solution(451371687744276982)
XLA Ops:
  7.2 0.8 compare_select_fusion
  8.0 0.7 compare_and_fusion
  8.7 7.5 %gather_fusion = f32[8,256,4,128]{3,2,1,0:T(4,128)} fusion(f32[12,256,4,128]{3,2,1,0:T(4,128)} %param.3, s32[1024]{0:T(1024)S(1)} %pad_clamp_fusion), kind=kCustom, calls=%fused_computation | custom fusion | bytes 8388640 | tf_op jit(solution)/shard_map/jit(_take)/gather | solution.py:9
  16.2 3.3 broadcast_select_fusion
  20.0 1.4 copy-done.1
  21.4 99.2 %all_to_all.15 = f32[8,256,4,128]{3,1,0,2:T(8,128)S(1)} all-to-all(f32[8,256,4,128]{3,1,0,2:T(8,128)S(1)} %copy.16), channel_id=1, replica_groups=mesh['gx'=2,'gy'=4,'gz'=4] {'gz'}, dimensions={2} | all-to-all | bytes 8388608 | tf_op jit(solution)/shard_map/all_to_all | solution.py:10
  121.1 14.8 %bitcast_multiply_fusion = f32[1024,1024]{1,0:T(8,128)} fusion(f32[8,1024,128]{2,1,0:T(8,128)S(1)} %bitcast.74), kind=kOutput, calls=%fused_computation.3 | convolution fusion | flops 12885950464 | bytes 8388608 | tf_op jit(solution)/shard_map/sxyz,swyz->xw/dot_general | solution.py:23
  136.1 141.0 %all-reduce.5.cloned.1.call-done = f32[1024,1024]{1,0:T(8,128)} async-done(((f32[1024,1024]{1,0:T(8,128)}), f32[1024,1024]{1,0:T(8,128)}) %all-reduce.5.cloned.1.call-update) | async-done | bytes 4194320 | tf_op jit(solution)/shard_map/psum | solution.py:22
  277.2 8.5 %fusion.27 = f32[1024,384]{1,0:T(8,128)S(1)} fusion(f32[1024,1024]{1,0:T(8,128)} %all-reduce.5.cloned.1.call-done, f32[1024,384]{1,0:T(8,128)S(1)} %copy-done), kind=kOutput, calls=%fused_computation.62 | convolution fusion | flops 4831838208 | bytes 7340032 | tf_op jit(solution)/shard_map/dot_general | solution.py:26
  285.7 3.5 fusion.28
  289.2 2.1 copy.18
  291.3 1.3 fusion.8
  292.6 0.8 copy-done.3
  293.5 11.7 %cholesky.77 = f32[128,128]{1,0:T(8,128)S(1)} custom-call(f32[128,128]{1,0:T(8,128)S(1)} %cholesky.192), custom_call_target="Cholesky" | custom-call | tf_op jit(solution)/shard_map/jit(cholesky)/cholesky | solution.py:28
  305.2 0.9 cholesky.169
  306.1 9.8 %custom-call.23 = f32[1,128,128]{1,2,0:T(8,128)S(1)} custom-call(f32[1,128,128]{2,1,0:T(8,128)S(1)} %get-tuple-element.36), custom_call_target="InvertDiagBlocksLowerTriangular" | custom-call | tf_op jit(solution)/shard_map/jit(cholesky)/cholesky | solution.py:28
  315.9 1.8 constant_dynamic-update-slice_fusion
  317.7 1.2 convolution_subtract_fusion.2
  318.9 12.1 %cholesky.162 = f32[128,128]{1,0:T(8,128)S(1)} custom-call(f32[128,128]{1,0:T(8,128)S(1)} %cholesky.196), custom_call_target="Cholesky" | custom-call | tf_op jit(solution)/shard_map/jit(cholesky)/cholesky | solution.py:28
  331.0 0.6 select_reduce_fusion.1
  331.6 9.8 %custom-call.24 = f32[1,128,128]{1,2,0:T(8,128)S(1)} custom-call(f32[1,128,128]{2,1,0:T(8,128)S(1)} %get-tuple-element.33), custom_call_target="InvertDiagBlocksLowerTriangular" | custom-call | tf_op jit(solution)/shard_map/jit(cholesky)/cholesky | solution.py:28
  341.5 0.8 convolution_dynamic-update-slice_fusion
  342.3 1.3 convolution_subtract_fusion.3
  343.6 11.7 %cholesky.181 = f32[128,128]{1,0:T(8,128)S(1)} custom-call(f32[128,128]{1,0:T(8,128)S(1)} %convolution_subtract_fusion.3), custom_call_target="Cholesky" | custom-call | tf_op jit(solution)/shard_map/jit(cholesky)/cholesky | solution.py:28
  355.3 0.6 select_reduce_fusion
  355.9 0.6 compare_reduce_fusion
  356.5 0.7 compare_reduce_fusion.1
  359.2 1.9 select_select_fusion
  361.1 10.2 %while.1 = (s32[]{:T(128)}, f32[384,384]{1,0:T(8,128)}, s32[3,2]{0,1:T(2,128)S(1)}, f32[3,128,128]{2,1,0:T(8,128)}, s32[]{:T(128)}) while((s32[]{:T(128)}, f32[384,384]{1,0:T(8,128)}, s32[3,2]{0,1:T(2,128)S(1)}, f32[3,128,128]{2,1,0:T(8,128)}, s32[]{:T(128)}) %tuple.32), condition=%wide.while_cond, body=%wide.while_body.sunk | while | flops 2 | bytes 132205 | solution.py:29
  361.2 0.5 fusion.40
  361.7 2.9 bitcast_dynamic-update-slice_fusion.2
  364.6 0.5 fusion.40
  365.2 2.8 bitcast_dynamic-update-slice_fusion.2
  368.6 2.8 bitcast_dynamic-update-slice_fusion.2
  371.4 30.5 %custom-call.25 = f32[3,128,128]{1,2,0:T(8,128)S(1)} custom-call(f32[3,128,128]{2,1,0:T(8,128)} %get-tuple-element.10), custom_call_target="InvertDiagBlocksLowerTriangular" | custom-call | tf_op jit(solution)/shard_map/jit(_solve_triangular)/triangular_solve | solution.py:29
  401.8 0.6 fusion.9
  402.5 1.8 convolution_subtract_fusion.1
  404.3 0.6 fusion.19
  405.0 3.1 convolution_subtract_fusion
  408.1 0.6 fusion.17
  408.9 15.1 %fusion.2 = f32[8,384,4,128]{1,3,2,0:T(8,128)} fusion(f32[8,256,4,128]{3,2,1,0:T(4,128)S(1)} %copy-done.2, f32[384,1024]{1,0:T(8,128)S(1)} %pad_maximum_fusion, s32[]{:T(128)S(6)} %select_n.24), kind=kOutput, calls=%fused_computation.6 | convolution fusion | flops 4831838208 | bytes 10878980 | tf_op jit(solution)/shard_map/xr,sxyz->sryz/dot_general | solution.py:37
  424.0 0.6 copy-done.4
  424.6 0.6 dynamic-slice.11
  425.3 0.7 copy.22
  426.0 1.6 constant_dynamic-slice_fusion.1
  427.6 218.3 %all-reduce.7.cloned.1.call-done = f32[8,384,4,128]{1,3,2,0:T(8,128)} async-done(((f32[8,384,4,128]{1,3,2,0:T(8,128)}), f32[8,384,4,128]{1,3,2,0:T(8,128)}) %all-reduce.7.cloned.1.call-update) | async-done | bytes 6291472
  645.9 2.2 constant_dynamic-slice_fusion.2
  648.0 2.8 copy.23
  (26 shorter events, 2.3 us)
Async XLA Ops:
  7.2 270.0 %copy-start = (f32[1024,384]{1,0:T(8,128)S(1)}, f32[1024,384]{1,0:T(8,128)}, u32[]{:S(2)}) copy-start(f32[1024,384]{1,0:T(8,128)} %param.5) | copy-start | bytes 4718596
  7.2 270.0 %all-reduce.5.cloned.1.call-start = ((), (), s32[]{:S(2)}) async-start(), calls=%async_computation.1 | async-start | bytes 8388608 | tf_op jit(solution)/shard_map/psum | solution.py:22
  19.5 1.9 copy-start.1
  135.9 510.0 %all-reduce.7.cloned.1.call-start = ((), (), s32[]{:S(2)}) async-start(), calls=%async_computation.2 | async-start | bytes 12582912
  292.6 0.8 copy-start.3
  404.3 4.6 copy-start.2
  424.0 0.7 copy-start.4
Sparse Core Ops, SparseCore 0:
  136.0 141.1 all-reduce.4
  424.1 221.7 all-reduce.6
where the time goes:
time: 667 us; the launch traced here: 658 us
  waiting for transfers between devices  359 us (54%)
  blocking collectives  99.2 us (15%)
  other arithmetic  96.4 us (14%)
  matrix products  53.8 us (8%)
  local copies, waits for them, and re-layouts  32.4 us (5%)
  between operations  16.4 us (2%)
    unnamed x3, waiting for transfers between devices  218 us
    psum x1, waiting for transfers between devices, per_device(): lax.psum(jnp.einsum('sxyz,swyz->xw', full_panel, full_panel, precision=hi...  141 us
    all_to_all x1, blocking collectives, per_device(): lax.all_to_all(picked, 'gz', split_axis=2, concat_axis=1, tiled=True)  99.2 us
    another operation x10, other arithmetic, per_device(): lower_factor = jnp.linalg.cholesky(inner_gram)  57.8 us
    another operation x4, other arithmetic, per_device(): jax.scipy.linalg.solve_triangular(lower_factor, image_full.T, lower=True)  32.6 us
    dot_general x1, matrix products, per_device(): projected = jnp.einsum('xr,sxyz->sryz', own_rows, picked, precision=highest)  15.1 us
    dot_general x1, matrix products, per_device(): jnp.einsum('sxyz,swyz->xw', full_panel, full_panel, precision=highest)  14.8 us
  transfers between devices with their start and end apart: 2, of which 2 were waited for; matrix products, arithmetic and copies ran while one was open for 0% of the time, Pallas kernels for 0%

commit v1 on v0

--- a/solution.py
+++ b/solution.py
@@ -19,10 +19,9 @@
     )
     scaling = 1.0 / column_total
     row_share = total_rows // lax.axis_size(("gx", "gy", "gz"))
-    gram_full = lax.psum(
-        jnp.einsum("sxyz,swyz->xw", full_panel, full_panel, precision=highest) * scaling,
-        ("gx", "gy", "gz"),
-    )
+    gram_full = jnp.einsum("sxyz,swyz->xw", full_panel, full_panel, precision=highest) * scaling
+    for name in (("gy", "gz"), "gx"):
+        gram_full = lax.psum(gram_full, name)
     image_full = jnp.dot(gram_full, basis_start, precision=highest)
     inner_gram = jnp.einsum("xr,xq->rq", image_full, image_full, precision=highest)
     lower_factor = jnp.linalg.cholesky(inner_gram)

time: 667 us -> 747 us (1.12)
  waiting for transfers between devices: 359 us -> 440 us
    psum x1 -> x2, waiting for transfers between devices: 141 us -> 220 us  [per_device(): gram_full = lax.psum(gram_full, name)]
    unnamed x3 -> x4, waiting for transfers between devices: 218 us -> 219 us
  transfers between devices with their start and end apart: 2 -> 3, of which waited for: 2 -> 3; matrix products, arithmetic and copies ran while one was open for 0% -> 0% of each run, Pallas kernels for 0% -> 0%
where the time goes in v1:
time: 747 us; the launch traced here: 738 us
  waiting for transfers between devices  440 us (59%)
  blocking collectives  99.2 us (13%)
  other arithmetic  96.4 us (13%)
  matrix products  53.8 us (7%)
  local copies, waits for them, and re-layouts  32.4 us (4%)
  between operations  16.1 us (2%)
    psum x2, waiting for transfers between devices, per_device(): gram_full = lax.psum(gram_full, name)  220 us
    unnamed x4, waiting for transfers between devices  219 us
    all_to_all x1, blocking collectives, per_device(): lax.all_to_all(picked, 'gz', split_axis=2, concat_axis=1, tiled=True)  99.2 us
    another operation x10, other arithmetic, per_device(): lower_factor = jnp.linalg.cholesky(inner_gram)  57.8 us
    another operation x4, other arithmetic, per_device(): jax.scipy.linalg.solve_triangular(lower_factor, image_full.T, lower=True)  32.6 us
    dot_general x1, matrix products, per_device(): projected = jnp.einsum('xr,sxyz->sryz', own_rows, picked, precision=highest)  15.1 us
  transfers between devices with their start and end apart: 3, of which 3 were waited for; matrix products, arithmetic and copies ran while one was open for 0% of the time, Pallas kernels for 0%

profile of v1, /device:TPU:0, one launch (start us, length us, event | category | flops | bytes accessed | tf_op | source)
XLA Modules:
  0.0 737.7 jit_solution(3390916554980197825)
XLA Ops:
  7.2 0.8 compare_select_fusion
  8.0 0.7 compare_and_fusion
  8.7 7.5 %gather_fusion = f32[8,256,4,128]{3,2,1,0:T(4,128)} fusion(f32[12,256,4,128]{3,2,1,0:T(4,128)} %param.3, s32[1024]{0:T(1024)S(1)} %pad_clamp_fusion), kind=kCustom, calls=%fused_computation | custom fusion | bytes 8388640 | tf_op jit(solution)/shard_map/jit(_take)/gather | solution.py:9
  16.2 3.3 broadcast_select_fusion
  20.0 1.4 copy-done.1
  21.4 99.2 %all_to_all.15 = f32[8,256,4,128]{3,1,0,2:T(8,128)S(1)} all-to-all(f32[8,256,4,128]{3,1,0,2:T(8,128)S(1)} %copy.16), channel_id=1, replica_groups=mesh['gx'=2,'gy'=4,'gz'=4] {'gz'}, dimensions={2} | all-to-all | bytes 8388608 | tf_op jit(solution)/shard_map/all_to_all | solution.py:10
  121.1 14.8 %bitcast_multiply_fusion = f32[1024,1024]{1,0:T(8,128)} fusion(f32[8,1024,128]{2,1,0:T(8,128)S(1)} %bitcast.74), kind=kOutput, calls=%fused_computation.3 | convolution fusion | flops 12885950464 | bytes 8388608 | tf_op jit(solution)/shard_map/sxyz,swyz->xw/dot_general | solution.py:22
  135.9 111.0 %all-reduce.6.cloned.1.call-done = f32[1024,1024]{1,0:T(8,128)} async-done(((f32[1024,1024]{1,0:T(8,128)}), f32[1024,1024]{1,0:T(8,128)}) %all-reduce.6.cloned.1.call-update) | async-done | bytes 4194320 | tf_op jit(solution)/shard_map/psum | solution.py:24
  247.1 109.1 %all-reduce.8.cloned.1.call-done = f32[1024,1024]{1,0:T(8,128)} async-done(((f32[1024,1024]{1,0:T(8,128)}), f32[1024,1024]{1,0:T(8,128)}) %all-reduce.8.cloned.1.call-update) | async-done | bytes 4194320 | tf_op jit(solution)/shard_map/psum | solution.py:24
  356.3 8.5 %fusion.27 = f32[1024,384]{1,0:T(8,128)S(1)} fusion(f32[1024,1024]{1,0:T(8,128)} %all-reduce.8.cloned.1.call-done, f32[1024,384]{1,0:T(8,128)S(1)} %copy-done), kind=kOutput, calls=%fused_computation.62 | convolution fusion | flops 4831838208 | bytes 7340032 | tf_op jit(solution)/shard_map/dot_general | solution.py:25
  364.8 3.5 fusion.28
  368.3 2.1 copy.18
  370.4 1.3 fusion.8
  371.7 0.8 copy-done.3
  372.5 11.7 %cholesky.77 = f32[128,128]{1,0:T(8,128)S(1)} custom-call(f32[128,128]{1,0:T(8,128)S(1)} %cholesky.192), custom_call_target="Cholesky" | custom-call | tf_op jit(solution)/shard_map/jit(cholesky)/cholesky | solution.py:27
  384.3 0.9 cholesky.169
  385.2 9.8 %custom-call.23 = f32[1,128,128]{1,2,0:T(8,128)S(1)} custom-call(f32[1,128,128]{2,1,0:T(8,128)S(1)} %get-tuple-element.36), custom_call_target="InvertDiagBlocksLowerTriangular" | custom-call | tf_op jit(solution)/shard_map/jit(cholesky)/cholesky | solution.py:27
  395.0 1.8 constant_dynamic-update-slice_fusion
  396.8 1.2 convolution_subtract_fusion.2
  398.0 12.1 %cholesky.162 = f32[128,128]{1,0:T(8,128)S(1)} custom-call(f32[128,128]{1,0:T(8,128)S(1)} %cholesky.196), custom_call_target="Cholesky" | custom-call | tf_op jit(solution)/shard_map/jit(cholesky)/cholesky | solution.py:27
  410.1 0.6 select_reduce_fusion.1
  410.7 9.8 %custom-call.24 = f32[1,128,128]{1,2,0:T(8,128)S(1)} custom-call(f32[1,128,128]{2,1,0:T(8,128)S(1)} %get-tuple-element.33), custom_call_target="InvertDiagBlocksLowerTriangular" | custom-call | tf_op jit(solution)/shard_map/jit(cholesky)/cholesky | solution.py:27
  420.5 0.8 convolution_dynamic-update-slice_fusion
  421.4 1.3 convolution_subtract_fusion.3
  422.6 11.7 %cholesky.181 = f32[128,128]{1,0:T(8,128)S(1)} custom-call(f32[128,128]{1,0:T(8,128)S(1)} %convolution_subtract_fusion.3), custom_call_target="Cholesky" | custom-call | tf_op jit(solution)/shard_map/jit(cholesky)/cholesky | solution.py:27
  434.4 0.6 select_reduce_fusion
  435.0 0.6 compare_reduce_fusion
  435.6 0.7 compare_reduce_fusion.1
  438.3 1.9 select_select_fusion
  440.2 10.2 %while.1 = (s32[]{:T(128)}, f32[384,384]{1,0:T(8,128)}, s32[3,2]{0,1:T(2,128)S(1)}, f32[3,128,128]{2,1,0:T(8,128)}, s32[]{:T(128)}) while((s32[]{:T(128)}, f32[384,384]{1,0:T(8,128)}, s32[3,2]{0,1:T(2,128)S(1)}, f32[3,128,128]{2,1,0:T(8,128)}, s32[]{:T(128)}) %tuple.32), condition=%wide.while_cond, body=%wide.while_body.sunk | while | flops 2 | bytes 132205 | solution.py:28
  440.3 0.5 fusion.40
  440.8 2.9 bitcast_dynamic-update-slice_fusion.2
  444.2 2.8 bitcast_dynamic-update-slice_fusion.2
  447.7 2.8 bitcast_dynamic-update-slice_fusion.2
  450.4 30.5 %custom-call.25 = f32[3,128,128]{1,2,0:T(8,128)S(1)} custom-call(f32[3,128,128]{2,1,0:T(8,128)} %get-tuple-element.10), custom_call_target="InvertDiagBlocksLowerTriangular" | custom-call | tf_op jit(solution)/shard_map/jit(_solve_triangular)/triangular_solve | solution.py:28
  480.9 0.6 fusion.9
  481.6 1.8 convolution_subtract_fusion.1
  483.4 0.6 fusion.19
  484.1 3.1 convolution_subtract_fusion
  487.2 0.6 fusion.17
  488.0 15.1 %fusion.2 = f32[8,384,4,128]{1,3,2,0:T(8,128)} fusion(f32[8,256,4,128]{3,2,1,0:T(4,128)S(1)} %copy-done.2, f32[384,1024]{1,0:T(8,128)S(1)} %pad_maximum_fusion, s32[]{:T(128)S(6)} %select_n.24), kind=kOutput, calls=%fused_computation.6 | convolution fusion | flops 4831838208 | bytes 10878980 | tf_op jit(solution)/shard_map/xr,sxyz->sryz/dot_general | solution.py:36
  503.1 0.6 copy-done.4
  503.7 0.6 dynamic-slice.11
  504.4 0.7 copy.22
  505.1 1.6 constant_dynamic-slice_fusion.1
  506.7 219.4 %all-reduce.10.cloned.1.call-done = f32[8,384,4,128]{1,3,2,0:T(8,128)} async-done(((f32[8,384,4,128]{1,3,2,0:T(8,128)}), f32[8,384,4,128]{1,3,2,0:T(8,128)}) %all-reduce.10.cloned.1.call-update) | async-done | bytes 6291472
  726.1 2.2 constant_dynamic-slice_fusion.2
  728.3 2.8 copy.23
  (29 shorter events, 2.9 us)
Async XLA Ops:
  7.2 349.1 %copy-start = (f32[1024,384]{1,0:T(8,128)S(1)}, f32[1024,384]{1,0:T(8,128)}, u32[]{:S(2)}) copy-start(f32[1024,384]{1,0:T(8,128)} %param.5) | copy-start | bytes 4718596
  7.2 239.7 %all-reduce.6.cloned.1.call-start = ((), (), s32[]{:S(2)}) async-start(), calls=%async_computation.1 | async-start | bytes 8388608 | tf_op jit(solution)/shard_map/psum | solution.py:24
  19.5 1.9 copy-start.1
  135.9 220.4 %all-reduce.8.cloned.1.call-start = ((), (), s32[]{:S(2)}) async-start(), calls=%async_computation.2 | async-start | bytes 8388608 | tf_op jit(solution)/shard_map/psum | solution.py:24
  246.9 479.2 %all-reduce.10.cloned.1.call-start = ((), (), s32[]{:S(2)}) async-start(), calls=%async_computation.3 | async-start | bytes 12582912
  371.7 0.8 copy-start.3
  483.4 4.6 copy-start.2
  503.0 0.7 copy-start.4
Sparse Core Ops, SparseCore 0:
  136.0 110.8 all-reduce.5
  249.4 106.7 all-reduce.7
  503.2 222.8 all-reduce.9
